TPU v7x, 128 devices: a whole 4x4x4 slice. The times are simulated.
128 devices in a mesh: tm: 32 (over x, y, core), chan: 4 (over z).
Axes of the slice: x: 4, y: 4, z: 4, core: 2. Of those that a mesh axis runs over, the one named last changes fastest.
Arguments:
- samples: float32 [64, 1048576], P('chan', 'tm'), may hold values from -6 to 6
- start_basis: float32 [512, 128], replicated, may hold values from -6 to 6
Outputs:
- factor: float32 [1024, 1024], P(('tm', 'chan'))
- states: float32 [128, 1048576], P(None, ('tm', 'chan'))
All inputs are finite; a program needn't handle non-finite values.
Results may differ from a plain program's by a relative error of at most 0.0003.
Values sent between devices are 32-bit elements; how exact they have to be, the bound alone decides.
No kernel may reach another device: no remote copies, remote signals or barrier semaphores. Data moves between devices by JAX's collectives and lax.ppermute only.
A program may use at most 256 MiB of HBM per device.

v0:
```python
import jax
import jax.numpy as jnp
from jax import lax
from jax.sharding import PartitionSpec as P

BR = 16
NSTEPS = 6


def from_behind(array, axis, by):
    size = lax.axis_size(axis)
    pairs = [(i, i + by) for i in range(size) if 0 <= i + by < size]
    return lax.ppermute(array, axis, pairs)


def upper_factor(gram):
    return jnp.linalg.cholesky(gram).T


def outer_gram(left, right):
    return lax.dot_general(
        left,
        right,
        (((1,), (1,)), ((), ())),
        precision=lax.Precision.HIGHEST,
        preferred_element_type=jnp.float32,
    )


def per_device(samples, start_basis):
    local = lax.all_to_all(samples, "chan", split_axis=1, concat_axis=0, tiled=True)
    count = local.shape[1]
    following = from_behind(local[:, : BR - 1], ("tm", "chan"), -1)
    extended = jnp.concatenate([local, following], 1)
    hankel = jnp.concatenate([extended[:, k : k + count] for k in range(BR)], 0)
    order = hankel.shape[0]
    half = order // 2
    total = count * lax.axis_size("tm") * lax.axis_size("chan")
    weight = 1.0 / (1.0 + jnp.mean(local * local, 0))
    gram = outer_gram(hankel * weight[None, :], hankel) * (1.0 / total)
    gram = lax.psum(gram, ("tm", "chan"))
    factor = upper_factor(gram)
    lead = jnp.dot(
        factor[half:, half:].T,
        start_basis,
        precision=lax.Precision.HIGHEST,
        preferred_element_type=jnp.float32,
    )
    basis = lead / jnp.sqrt(jnp.sum(lead * lead))
    for step in range(NSTEPS):
        inner = jnp.dot(
            basis.T, basis, precision=lax.Precision.HIGHEST, preferred_element_type=jnp.float32
        )
        basis = 1.5 * basis - 0.5 * jnp.dot(
            basis, inner, precision=lax.Precision.HIGHEST, preferred_element_type=jnp.float32
        )
    states = jnp.dot(
        basis.T, hankel[half:], precision=lax.Precision.HIGHEST, preferred_element_type=jnp.float32
    )
    share = order // (lax.axis_size("tm") * lax.axis_size("chan"))
    position = lax.axis_index(("tm", "chan"))
    mine = lax.dynamic_slice_in_dim(factor, position * share, share, 0)
    return (mine, states)


def solution(mesh):
    placed = (P("chan", "tm"), P())
    return jax.shard_map(
        per_device,
        mesh=mesh,
        in_specs=placed,
        out_specs=(P(("tm", "chan"), None), P(None, ("tm", "chan"))),
        check_vma=False,
    )
```

profile of v0, /device:TPU:1, one launch (start us, length us, event | category | flops | bytes accessed | tf_op | source)
XLA Modules:
  0.0 616.3 jit_solution(9280351724594159771)
XLA Ops:
  7.2 1.8 copy.55
  9.0 31.1 %all_to_all.19 = f32[16,4,8192]{2,0,1:T(8,128)S(1)} all-to-all(f32[16,4,8192]{2,0,1:T(8,128)S(1)} %bitcast.102), channel_id=1, replica_groups=mesh['tm'=32,'chan'=4] {'chan'}, dimensions={1} | all-to-all | bytes 4194304 | tf_op jit(solution)/shard_map/all_to_all | solution.py:31
  40.1 4.5 collective-permute-start
  44.9 0.8 collective-permute-done
  48.7 2.1 fusion.53
  50.8 2.5 fusion.65
  53.2 1.9 fusion.11
  55.2 2.0 fusion.13
  57.1 2.0 fusion.15
  59.1 1.9 fusion.17
  61.1 2.0 fusion.19
  63.0 1.9 fusion.21
  65.0 2.0 fusion.64
  66.9 1.9 fusion.62
  68.9 1.9 fusion.60
  70.8 2.0 fusion.58
  72.8 2.0 fusion.56
  74.8 1.9 fusion.54
  76.7 2.0 fusion.66
  78.6 2.2 fusion.30
  80.8 5.7 copy-done.2
  86.5 118.2 %fusion.4 = f32[1024,1024]{0,1:T(8,128)} fusion(f32[1024,8192]{1,0:T(8,128)} %get-tuple-element.11, f32[8192]{0:T(1024)S(1)} %add_divide_fusion), kind=kOutput, calls=%fused_computation.21 | convolution fusion | flops 103088652288 | bytes 37781504 | tf_op jit(solution)/shard_map/dot_general | solution.py:21
  204.7 157.1 %all-reduce.3.cloned.1.call-done = f32[1024,1024]{0,1:T(8,128)} async-done(((f32[1024,1024]{0,1:T(8,128)}), f32[1024,1024]{0,1:T(8,128)}) %all-reduce.3.cloned.1.call-update) | async-done | bytes 4194320 | tf_op jit(solution)/shard_map/psum | solution.py:41
  361.8 5.3 copy.37
  367.2 4.4 fusion.3
  371.6 2.0 copy-done.3
  373.6 11.7 %cholesky.223 = f32[128,128]{1,0:T(8,128)S(1)} custom-call(f32[128,128]{1,0:T(8,128)S(1)} %cholesky.580), custom_call_target="Cholesky" | custom-call | tf_op jit(solution)/shard_map/jit(cholesky)/cholesky | solution.py:17
  385.4 9.8 %custom-call.59 = f32[1,128,128]{1,2,0:T(8,128)S(1)} custom-call(f32[1,128,128]{2,1,0:T(8,128)S(1)} %get-tuple-element.37), custom_call_target="InvertDiagBlocksLowerTriangular" | custom-call | tf_op jit(solution)/shard_map/jit(cholesky)/cholesky | solution.py:17
  395.2 1.6 fusion.51
  397.0 1.9 slice_subtract_fusion
  399.0 2.5 cholesky.255
  401.4 12.1 %cholesky.244 = f32[128,128]{1,0:T(8,128)S(1)} custom-call(f32[128,128]{1,0:T(8,128)S(1)} %cholesky.584), custom_call_target="Cholesky" | custom-call | tf_op jit(solution)/shard_map/jit(cholesky)/cholesky | solution.py:17
  413.5 0.9 constant_dynamic-update-slice_fusion.7
  415.1 9.8 %custom-call.60 = f32[1,128,128]{1,2,0:T(8,128)S(1)} custom-call(f32[1,128,128]{2,1,0:T(8,128)S(1)} %get-tuple-element.34), custom_call_target="InvertDiagBlocksLowerTriangular" | custom-call | tf_op jit(solution)/shard_map/jit(cholesky)/cholesky | solution.py:17
  424.9 1.3 convolution_dynamic-update-slice_fusion
  426.1 2.1 slice_subtract_fusion.1
  428.3 11.7 %cholesky.468 = f32[128,128]{1,0:T(8,128)S(1)} custom-call(f32[128,128]{1,0:T(8,128)S(1)} %cholesky.589), custom_call_target="Cholesky" | custom-call | tf_op jit(solution)/shard_map/jit(cholesky)/cholesky | solution.py:17
  441.3 9.8 %custom-call.61 = f32[1,128,128]{1,2,0:T(8,128)S(1)} custom-call(f32[1,128,128]{2,1,0:T(8,128)S(1)} %get-tuple-element.31), custom_call_target="InvertDiagBlocksLowerTriangular" | custom-call | tf_op jit(solution)/shard_map/jit(cholesky)/cholesky | solution.py:17
  451.1 1.2 convolution_dynamic-update-slice_fusion.1
  452.3 2.3 slice_subtract_fusion.2
  454.6 11.9 %cholesky.487 = f32[128,128]{1,0:T(8,128)S(1)} custom-call(f32[128,128]{1,0:T(8,128)S(1)} %cholesky.594), custom_call_target="Cholesky" | custom-call | tf_op jit(solution)/shard_map/jit(cholesky)/cholesky | solution.py:17
  467.8 9.8 %custom-call.62 = f32[1,128,128]{1,2,0:T(8,128)S(1)} custom-call(f32[1,128,128]{2,1,0:T(8,128)S(1)} %get-tuple-element.28), custom_call_target="InvertDiagBlocksLowerTriangular" | custom-call | tf_op jit(solution)/shard_map/jit(cholesky)/cholesky | solution.py:17
  477.6 1.1 convolution_dynamic-update-slice_fusion.2
  478.7 2.3 slice_subtract_fusion.3
  481.1 11.7 %cholesky.506 = f32[128,128]{1,0:T(8,128)S(1)} custom-call(f32[128,128]{1,0:T(8,128)S(1)} %cholesky.599), custom_call_target="Cholesky" | custom-call | tf_op jit(solution)/shard_map/jit(cholesky)/cholesky | solution.py:17
  493.4 0.7 compare_reduce_fusion.3
  494.1 10.0 %custom-call.63 = f32[1,128,128]{1,2,0:T(8,128)S(1)} custom-call(f32[1,128,128]{2,1,0:T(8,128)S(1)} %get-tuple-element.25), custom_call_target="InvertDiagBlocksLowerTriangular" | custom-call | tf_op jit(solution)/shard_map/jit(cholesky)/cholesky | solution.py:17
  504.1 1.0 convolution_dynamic-update-slice_fusion.3
  505.2 2.3 slice_subtract_fusion.4
  507.4 11.7 %cholesky.526 = f32[128,128]{1,0:T(8,128)S(1)} custom-call(f32[128,128]{1,0:T(8,128)S(1)} %cholesky.604), custom_call_target="Cholesky" | custom-call | tf_op jit(solution)/shard_map/jit(cholesky)/cholesky | solution.py:17
  520.4 9.8 %custom-call.64 = f32[1,128,128]{1,2,0:T(8,128)S(1)} custom-call(f32[1,128,128]{2,1,0:T(8,128)S(1)} %get-tuple-element.22), custom_call_target="InvertDiagBlocksLowerTriangular" | custom-call | tf_op jit(solution)/shard_map/jit(cholesky)/cholesky | solution.py:17
  530.3 0.9 convolution_dynamic-update-slice_fusion.4
  531.2 2.0 slice_subtract_fusion.5
  533.3 12.1 %cholesky.546 = f32[128,128]{1,0:T(8,128)S(1)} custom-call(f32[128,128]{1,0:T(8,128)S(1)} %cholesky.609), custom_call_target="Cholesky" | custom-call | tf_op jit(solution)/shard_map/jit(cholesky)/cholesky | solution.py:17
  546.6 9.8 %custom-call.65 = f32[1,128,128]{1,2,0:T(8,128)S(1)} custom-call(f32[1,128,128]{2,1,0:T(8,128)S(1)} %get-tuple-element.19), custom_call_target="InvertDiagBlocksLowerTriangular" | custom-call | tf_op jit(solution)/shard_map/jit(cholesky)/cholesky | solution.py:17
  556.4 0.9 convolution_dynamic-update-slice_fusion.5
  557.3 1.8 slice_subtract_fusion.6
  559.1 11.7 %cholesky.564 = f32[128,128]{1,0:T(8,128)S(1)} custom-call(f32[128,128]{1,0:T(8,128)S(1)} %slice_subtract_fusion.6), custom_call_target="Cholesky" | custom-call | tf_op jit(solution)/shard_map/jit(cholesky)/cholesky | solution.py:17
  577.8 2.8 fusion.130
  581.2 2.5 select_select_fusion
  583.7 1.6 multiply_reduce_fusion
  592.0 1.2 dynamic-slice_bitcast_fusion
  593.3 0.8 copy.45
  594.0 15.2 %fusion.103 = f32[128,8192]{1,0:T(8,128)} fusion(f32[512,128]{1,0:T(8,128)S(1)} %fusion.31, f32[512,8192]{1,0:T(8,128)} %copy-done.2), kind=kOutput, calls=%fused_computation.168 | convolution fusion | flops 6442450944 | bytes 21233664 | tf_op jit(solution)/shard_map/dot_general | solution.py:57
  (50 shorter events, 18.6 us)
Async XLA Ops:
  7.2 576.6 %copy-start = (f32[512,128]{1,0:T(8,128)S(1)}, f32[512,128]{1,0:T(8,128)}, u32[]{:S(2)}) copy-start(f32[512,128]{1,0:T(8,128)} %param.3) | copy-start | bytes 786436
  7.2 354.6 %all-reduce.3.cloned.1.call-start = ((), (), s32[]{:S(2)}) async-start(), calls=%async_computation.1 | async-start | bytes 8388608 | tf_op jit(solution)/shard_map/psum | solution.py:41
  40.1 5.5 collective-permute-start
  80.8 5.7 copy-start.2
  371.6 2.0 copy-start.3
  577.8 3.5 copy-start.1
Sparse Core Ops, SparseCore 0:
  204.8 156.9 all-reduce.2
where the time goes:
time: 626 us; the launch traced here: 616 us
  other arithmetic  218 us (35%)
  matrix products  164 us (26%)
  waiting for transfers between devices  158 us (25%)
  blocking collectives  31.1 us (5%)
  local copies, waits for them, and re-layouts  21.1 us (3%)
  between operations  20.2 us (3%)
    another operation x30, other arithmetic, upper_factor(): return jnp.linalg.cholesky(gram).T  173 us
    psum x1, waiting for transfers between devices, per_device(): gram = lax.psum(gram, ('tm', 'chan'))  157 us
    dot_general x1, matrix products, outer_gram(): lax.dot_general(left, right, (((1,), (1,)), ((), ())), precision=lax.Prec...  118 us
    unnamed x20, other arithmetic  33 us
    all_to_all x1, blocking collectives, per_device(): lax.all_to_all(samples, 'chan', split_axis=1, concat_axis=0, tiled=True)  31.1 us
    another operation x14, matrix products, upper_factor(): return jnp.linalg.cholesky(gram).T  22.8 us
    dot_general x1, matrix products, per_device(): jnp.dot(basis.T, hankel[half:], precision=lax.Precision.HIGHEST, preferre...  15.2 us
  transfers between devices with their start and end apart: 2, of which 2 were waited for; matrix products, arithmetic and copies ran while one was open for 0% of the time, Pallas kernels for 0%

commit v1 on v0

--- a/solution.py
+++ b/solution.py
@@ -38,7 +38,10 @@
     total = count * lax.axis_size("tm") * lax.axis_size("chan")
     weight = 1.0 / (1.0 + jnp.mean(local * local, 0))
     gram = outer_gram(hankel * weight[None, :], hankel) * (1.0 / total)
-    gram = lax.psum(gram, ("tm", "chan"))
+    _recast_loads = lambda page, lane_axis, peer_axis: lax.psum(
+        lax.psum(page, lane_axis), peer_axis
+    )
+    gram = _recast_loads(gram, "chan", "tm")
     factor = upper_factor(gram)
     lead = jnp.dot(
         factor[half:, half:].T,

time: 626 us -> 679 us (1.085)
  waiting for transfers between devices: 158 us -> 212 us
    psum x1 -> x2, waiting for transfers between devices: 157 us -> 211 us  [the longest x1 115 us: per_device(): lax.psum(lax.psum(page, lane_axis), peer_axis)]
  transfers between devices with their start and end apart: 2 -> 3, of which waited for: 2 -> 3; matrix products, arithmetic and copies ran while one was open for 0% -> 0% of each run, Pallas kernels for 0% -> 0%
where the time goes in v1:
time: 679 us; the launch traced here: 670 us
  other arithmetic  218 us (32%)
  waiting for transfers between devices  212 us (31%)
  matrix products  164 us (24%)
  blocking collectives  31.1 us (5%)
  local copies, waits for them, and re-layouts  21.1 us (3%)
  between operations  20.3 us (3%)
    another operation x30, other arithmetic, upper_factor(): return jnp.linalg.cholesky(gram).T  173 us
    dot_general x1, matrix products, outer_gram(): lax.dot_general(left, right, (((1,), (1,)), ((), ())), precision=lax.Prec...  118 us
    psum x1, waiting for transfers between devices, per_device(): lax.psum(lax.psum(page, lane_axis), peer_axis)  115 us
    psum x1, waiting for transfers between devices, per_device(): lax.psum(page, lane_axis)  95.9 us
    unnamed x20, other arithmetic  33 us
    all_to_all x1, blocking collectives, per_device(): lax.all_to_all(samples, 'chan', split_axis=1, concat_axis=0, tiled=True)  31.1 us
    another operation x14, matrix products, upper_factor(): return jnp.linalg.cholesky(gram).T  22.8 us
    dot_general x1, matrix products, per_device(): jnp.dot(basis.T, hankel[half:], precision=lax.Precision.HIGHEST, preferre...  15.2 us
  transfers between devices with their start and end apart: 3, of which 3 were waited for; matrix products, arithmetic and copies ran while one was open for 0% of the time, Pallas kernels for 0%

profile of v1, /device:TPU:1, one launch (start us, length us, event | category | flops | bytes accessed | tf_op | source)
XLA Modules:
  0.0 670.0 jit_solution(18112390807650637938)
XLA Ops:
  7.2 1.8 copy.55
  9.0 31.1 %all_to_all.19 = f32[16,4,8192]{2,0,1:T(8,128)S(1)} all-to-all(f32[16,4,8192]{2,0,1:T(8,128)S(1)} %bitcast.102), channel_id=1, replica_groups=mesh['tm'=32,'chan'=4] {'chan'}, dimensions={1} | all-to-all | bytes 4194304 | tf_op jit(solution)/shard_map/all_to_all | solution.py:31
  40.1 4.5 collective-permute-start
  44.9 0.8 collective-permute-done
  48.7 2.1 fusion.47
  50.8 2.5 fusion.59
  53.2 1.9 fusion.11
  55.2 2.0 fusion.13
  57.1 2.0 fusion.15
  59.1 1.9 fusion.17
  61.1 2.0 fusion.19
  63.0 1.9 fusion.21
  65.0 2.0 fusion.58
  66.9 1.9 fusion.56
  68.9 1.9 fusion.54
  70.8 2.0 fusion.52
  72.8 2.0 fusion.50
  74.8 1.9 fusion.48
  76.7 2.0 fusion.60
  78.6 2.2 fusion.30
  80.8 5.7 copy-done.2
  86.5 118.2 %fusion.4 = f32[1024,1024]{0,1:T(8,128)} fusion(f32[1024,8192]{1,0:T(8,128)} %get-tuple-element.11, f32[8192]{0:T(1024)S(1)} %add_divide_fusion), kind=kOutput, calls=%fused_computation.21 | convolution fusion | flops 103088652288 | bytes 37781504 | tf_op jit(solution)/shard_map/dot_general | solution.py:21
  204.7 95.9 %all-reduce.4.cloned.1.call-done = f32[1024,1024]{0,1:T(8,128)} async-done(((f32[1024,1024]{0,1:T(8,128)}), f32[1024,1024]{0,1:T(8,128)}) %all-reduce.4.cloned.1.call-update) | async-done | bytes 4194320 | tf_op jit(solution)/shard_map/psum | solution.py:42
  300.7 114.9 %all-reduce.6.cloned.1.call-done = f32[1024,1024]{0,1:T(8,128)} async-done(((f32[1024,1024]{0,1:T(8,128)}), f32[1024,1024]{0,1:T(8,128)}) %all-reduce.6.cloned.1.call-update) | async-done | bytes 4194320 | tf_op jit(solution)/shard_map/psum | solution.py:41
  415.6 5.3 copy.37
  420.9 4.4 fusion.3
  425.3 2.0 copy-done.3
  427.4 11.7 %cholesky.223 = f32[128,128]{1,0:T(8,128)S(1)} custom-call(f32[128,128]{1,0:T(8,128)S(1)} %cholesky.580), custom_call_target="Cholesky" | custom-call | tf_op jit(solution)/shard_map/jit(cholesky)/cholesky | solution.py:17
  439.1 9.8 %custom-call.59 = f32[1,128,128]{1,2,0:T(8,128)S(1)} custom-call(f32[1,128,128]{2,1,0:T(8,128)S(1)} %get-tuple-element.37), custom_call_target="InvertDiagBlocksLowerTriangular" | custom-call | tf_op jit(solution)/shard_map/jit(cholesky)/cholesky | solution.py:17
  448.9 1.6 fusion.45
  450.8 1.9 convolution_subtract_fusion
  452.7 2.5 cholesky.255
  455.2 12.1 %cholesky.244 = f32[128,128]{1,0:T(8,128)S(1)} custom-call(f32[128,128]{1,0:T(8,128)S(1)} %cholesky.584), custom_call_target="Cholesky" | custom-call | tf_op jit(solution)/shard_map/jit(cholesky)/cholesky | solution.py:17
  467.3 0.9 constant_dynamic-update-slice_fusion.7
  468.8 9.8 %custom-call.60 = f32[1,128,128]{1,2,0:T(8,128)S(1)} custom-call(f32[1,128,128]{2,1,0:T(8,128)S(1)} %get-tuple-element.34), custom_call_target="InvertDiagBlocksLowerTriangular" | custom-call | tf_op jit(solution)/shard_map/jit(cholesky)/cholesky | solution.py:17
  478.6 1.3 convolution_dynamic-update-slice_fusion
  479.9 2.1 convolution_subtract_fusion.1
  482.0 11.7 %cholesky.468 = f32[128,128]{1,0:T(8,128)S(1)} custom-call(f32[128,128]{1,0:T(8,128)S(1)} %cholesky.589), custom_call_target="Cholesky" | custom-call | tf_op jit(solution)/shard_map/jit(cholesky)/cholesky | solution.py:17
  495.0 9.8 %custom-call.61 = f32[1,128,128]{1,2,0:T(8,128)S(1)} custom-call(f32[1,128,128]{2,1,0:T(8,128)S(1)} %get-tuple-element.31), custom_call_target="InvertDiagBlocksLowerTriangular" | custom-call | tf_op jit(solution)/shard_map/jit(cholesky)/cholesky | solution.py:17
  504.8 1.2 convolution_dynamic-update-slice_fusion.1
  506.0 2.3 convolution_subtract_fusion.2
  508.4 11.9 %cholesky.487 = f32[128,128]{1,0:T(8,128)S(1)} custom-call(f32[128,128]{1,0:T(8,128)S(1)} %cholesky.594), custom_call_target="Cholesky" | custom-call | tf_op jit(solution)/shard_map/jit(cholesky)/cholesky | solution.py:17
  521.5 9.8 %custom-call.62 = f32[1,128,128]{1,2,0:T(8,128)S(1)} custom-call(f32[1,128,128]{2,1,0:T(8,128)S(1)} %get-tuple-element.28), custom_call_target="InvertDiagBlocksLowerTriangular" | custom-call | tf_op jit(solution)/shard_map/jit(cholesky)/cholesky | solution.py:17
  531.4 1.1 convolution_dynamic-update-slice_fusion.2
  532.4 2.3 convolution_subtract_fusion.3
  534.8 11.7 %cholesky.506 = f32[128,128]{1,0:T(8,128)S(1)} custom-call(f32[128,128]{1,0:T(8,128)S(1)} %cholesky.599), custom_call_target="Cholesky" | custom-call | tf_op jit(solution)/shard_map/jit(cholesky)/cholesky | solution.py:17
  547.9 10.0 %custom-call.63 = f32[1,128,128]{1,2,0:T(8,128)S(1)} custom-call(f32[1,128,128]{2,1,0:T(8,128)S(1)} %get-tuple-element.25), custom_call_target="InvertDiagBlocksLowerTriangular" | custom-call | tf_op jit(solution)/shard_map/jit(cholesky)/cholesky | solution.py:17
  557.9 1.0 convolution_dynamic-update-slice_fusion.3
  558.9 2.3 convolution_subtract_fusion.4
  561.2 11.7 %cholesky.526 = f32[128,128]{1,0:T(8,128)S(1)} custom-call(f32[128,128]{1,0:T(8,128)S(1)} %cholesky.604), custom_call_target="Cholesky" | custom-call | tf_op jit(solution)/shard_map/jit(cholesky)/cholesky | solution.py:17
  574.2 9.8 %custom-call.64 = f32[1,128,128]{1,2,0:T(8,128)S(1)} custom-call(f32[1,128,128]{2,1,0:T(8,128)S(1)} %get-tuple-element.22), custom_call_target="InvertDiagBlocksLowerTriangular" | custom-call | tf_op jit(solution)/shard_map/jit(cholesky)/cholesky | solution.py:17
  584.0 0.9 convolution_dynamic-update-slice_fusion.4
  584.9 2.0 convolution_subtract_fusion.5
  587.0 12.1 %cholesky.546 = f32[128,128]{1,0:T(8,128)S(1)} custom-call(f32[128,128]{1,0:T(8,128)S(1)} %cholesky.609), custom_call_target="Cholesky" | custom-call | tf_op jit(solution)/shard_map/jit(cholesky)/cholesky | solution.py:17
  600.4 9.8 %custom-call.65 = f32[1,128,128]{1,2,0:T(8,128)S(1)} custom-call(f32[1,128,128]{2,1,0:T(8,128)S(1)} %get-tuple-element.19), custom_call_target="InvertDiagBlocksLowerTriangular" | custom-call | tf_op jit(solution)/shard_map/jit(cholesky)/cholesky | solution.py:17
  610.2 0.9 convolution_dynamic-update-slice_fusion.5
  611.0 1.8 convolution_subtract_fusion.6
  612.8 11.7 %cholesky.564 = f32[128,128]{1,0:T(8,128)S(1)} custom-call(f32[128,128]{1,0:T(8,128)S(1)} %convolution_subtract_fusion.6), custom_call_target="Cholesky" | custom-call | tf_op jit(solution)/shard_map/jit(cholesky)/cholesky | solution.py:17
  631.5 2.8 fusion.113
  635.0 2.5 select_select_fusion
  637.5 1.6 multiply_reduce_fusion
  645.7 1.2 dynamic-slice_bitcast_fusion
  647.0 0.8 copy.45
  647.8 15.2 %fusion.86 = f32[128,8192]{1,0:T(8,128)} fusion(f32[512,128]{1,0:T(8,128)S(1)} %fusion.31, f32[512,8192]{1,0:T(8,128)} %copy-done.2), kind=kOutput, calls=%fused_computation.161 | convolution fusion | flops 6442450944 | bytes 21233664 | tf_op jit(solution)/shard_map/dot_general | solution.py:60
  (53 shorter events, 19.4 us)
Async XLA Ops:
  7.2 630.3 %copy-start = (f32[512,128]{1,0:T(8,128)S(1)}, f32[512,128]{1,0:T(8,128)}, u32[]{:S(2)}) copy-start(f32[512,128]{1,0:T(8,128)} %param.3) | copy-start | bytes 786436
  7.2 293.5 %all-reduce.4.cloned.1.call-start = ((), (), s32[]{:S(2)}) async-start(), calls=%async_computation.1 | async-start | bytes 8388608 | tf_op jit(solution)/shard_map/psum | solution.py:42
  40.1 5.5 collective-permute-start
  80.8 5.7 copy-start.2
  204.7 210.9 %all-reduce.6.cloned.1.call-start = ((), (), s32[]{:S(2)}) async-start(), calls=%async_computation.2 | async-start | bytes 8388608 | tf_op jit(solution)/shard_map/psum | solution.py:41
  425.3 2.0 copy-start.3
  631.5 3.5 copy-start.1
Sparse Core Ops, SparseCore 0:
  204.8 95.8 all-reduce.3
  304.3 111.1 all-reduce.5
